TPU v7x, 32 devices: a whole 2x2x4 slice. The times are simulated.
32 devices in a mesh: row: 16 (over z, x, core), col: 2 (over y).
Axes of the slice: x: 2, y: 2, z: 4, core: 2. Of those that a mesh axis runs over, the one named last changes fastest.
Arguments:
- counts: int32 [8192, 32768], P('row', 'col'), may hold values from 0 to 63
- row_support: int32 [8192], P(('row', 'col')), may hold values from 1 to 2209
- col_support: int32 [32768], P(('col', 'row')), may hold values from 1 to 2209
- total: int32 [1], replicated, may hold values from 256 to 4095
- sketch: bfloat16 [32768, 256], P('col'), may hold values from -6 to 6
Outputs:
- left_basis: float32 [8192, 256], P('row')
- right_basis: float32 [32768, 256], P('col')
All inputs are finite; a program needn't handle non-finite values.
Results may differ from a plain program's by a relative error of at most 0.012.
Values may be sent and summed in bfloat16 or wider, within the bound.
A program may use at most 192 MiB of HBM per device.

v0:
```python
import jax
import jax.numpy as jnp
from jax import lax
from jax.sharding import PartitionSpec as P


def lift(block, row_part, col_part, total):
    value = jnp.log(jnp.maximum(block, 1).astype(jnp.float32))
    value = value + jnp.log(total[0].astype(jnp.float32))
    value = value - jnp.log(row_part.astype(jnp.float32))[:, None]
    value = value - jnp.log(col_part.astype(jnp.float32))[None, :]
    return jnp.where(block > 0, jnp.maximum(value, 0.0), 0.0).astype(jnp.bfloat16)


def factor_of(gram):
    return jnp.linalg.cholesky(gram)


def solve_rows(lower, matrix):
    return jax.scipy.linalg.solve_triangular(lower, matrix.T, lower=True).T


def gram_of(matrix):
    return jnp.dot(matrix.T, matrix, precision=lax.Precision.HIGHEST)


def per_device(counts, row_support, col_support, total, sketch):
    row_local = lax.all_gather(row_support, "col", axis=0, tiled=True)
    col_local = lax.all_gather(col_support, "row", axis=0, tiled=True)
    table = lift(counts, row_local, col_local, total)
    row_count = table.shape[0]
    col_count = table.shape[1]

    def left_orth(rhs, narrow):
        whole = lax.psum(jnp.dot(table, rhs, preferred_element_type=jnp.float32), "col")
        gram = lax.psum(gram_of(whole), "row")
        basis = solve_rows(factor_of(gram), whole)
        if narrow:
            return basis.astype(jnp.bfloat16)
        return basis

    q_first = left_orth(sketch, True)
    partial_value = lax.dot_general(
        table, q_first, (((0,), (0,)), ((), ())), preferred_element_type=jnp.float32
    )
    whole = lax.psum(partial_value, "row")
    gram = lax.psum(gram_of(whole), "col")
    q_second = solve_rows(factor_of(gram), whole)
    q_third = left_orth(q_second.astype(jnp.bfloat16), False)
    total_rows = row_count * lax.axis_size("row")
    total_cols = col_count * lax.axis_size("col")
    return (
        q_third * jnp.sqrt(jnp.float32(total_rows)),
        q_second * jnp.sqrt(jnp.float32(total_cols)),
    )


def solution(mesh):
    in_specs = (P("row", "col"), P(("row", "col")), P(("col", "row")), P(), P("col", None))
    out_specs = (P("row", None), P("col", None))
    return jax.shard_map(
        per_device, mesh=mesh, in_specs=in_specs, out_specs=out_specs, check_vma=False
    )
```

profile of v0, /device:TPU:0, one launch (start us, length us, event | category | flops | bytes accessed | tf_op | source)
XLA Modules:
  0.0 932.7 jit_solution(9221446948077840741)
XLA Ops:
  7.2 23.5 %all_gather.7 = s32[16384]{0:T(1024)S(1)} all-gather(s32[1024]{0:T(1024)} %param.10), channel_id=1, replica_groups=mesh['row'=16,'col'=2] {'row'}, dimensions={0}, use_global_device_ids=true | all-gather | bytes 69632 | tf_op jit(solution)/shard_map/all_gather | solution.py:29
  35.9 17.1 %select_convert_fusion = bf16[512,16384]{1,0:T(8,128)(2,1)S(1)} fusion(s32[512,16384]{1,0:T(8,128)} %param.8, f32[16384]{0:T(1024)S(1)} %convert_log_fusion, f32[512]{0:T(512)S(1)} %bitcast.119, f32[]{:T(128)} %bitcast), kind=kLoop, calls=%fused_computation.6 | loop fusion | flops 75497472 | bytes 50399236 | tf_op jit(solution)/shard_map/convert_element_type | solution.py:12
  67.0 26.0 %all-reduce.8.cloned.1.call-done = f32[512,256]{1,0:T(8,128)} async-done(((f32[512,256]{1,0:T(8,128)}), f32[512,256]{1,0:T(8,128)}) %all-reduce.8.cloned.1.call-update) | async-done | bytes 524304 | tf_op jit(solution)/shard_map/psum | solution.py:35
  96.2 90.5 %all-reduce.10.cloned.1.call-done = f32[256,256]{0,1:T(8,128)} async-done(((f32[256,256]{0,1:T(8,128)}), f32[256,256]{0,1:T(8,128)}) %all-reduce.10.cloned.1.call-update) | async-done | bytes 262160 | tf_op jit(solution)/shard_map/psum | solution.py:36
  188.8 11.7 %cholesky.172 = f32[128,128]{1,0:T(8,128)S(1)} custom-call(f32[128,128]{1,0:T(8,128)S(1)} %cholesky.270), custom_call_target="Cholesky" | custom-call | tf_op jit(solution)/shard_map/jit(cholesky)/cholesky | solution.py:16
  210.9 11.7 %cholesky.189 = f32[128,128]{1,0:T(8,128)S(1)} custom-call(f32[128,128]{1,0:T(8,128)S(1)} %convolution_subtract_fusion.5), custom_call_target="Cholesky" | custom-call | tf_op jit(solution)/shard_map/jit(cholesky)/cholesky | solution.py:16
  229.4 19.7 %custom-call.20 = f32[2,128,128]{1,2,0:T(8,128)S(1)} custom-call(f32[2,128,128]{2,1,0:T(8,128)S(1)} %get-tuple-element.26), custom_call_target="InvertDiagBlocksLowerTriangular" | custom-call | tf_op jit(solution)/shard_map/jit(_solve_triangular)/triangular_solve | solution.py:20
  252.4 16.1 %fusion.6 = f32[16384,256]{1,0:T(8,128)} fusion(bf16[512,16384]{1,0:T(8,128)(2,1)} %copy-done.2, bf16[128,512]{1,0:T(8,128)(2,1)S(1)} %fusion.23, f32[128,512]{1,0:T(8,128)S(1)} %fusion.9), kind=kOutput, calls=%fused_computation.25 | convolution fusion | flops 4295491584 | bytes 33947648 | tf_op jit(solution)/shard_map/dot_general | solution.py:43
  268.6 298.5 %all-reduce.12.cloned.1.call-done = f32[16384,256]{1,0:T(8,128)} async-done(((f32[16384,256]{1,0:T(8,128)}), f32[16384,256]{1,0:T(8,128)}) %all-reduce.12.cloned.1.call-update) | async-done | bytes 16777232 | tf_op jit(solution)/shard_map/psum | solution.py:46
  567.1 37.8 %fusion.44 = f32[256,256]{0,1:T(8,128)} fusion(f32[16384,256]{1,0:T(8,128)} %all-reduce.12.cloned.1.call-done), kind=kOutput, calls=%fused_computation.95 | convolution fusion | flops 12884901888 | bytes 17039360 | tf_op jit(solution)/shard_map/dot_general | solution.py:24
  605.0 23.0 %all-reduce.14.cloned.1.call-done = f32[256,256]{0,1:T(8,128)} async-done(((f32[256,256]{0,1:T(8,128)}), f32[256,256]{0,1:T(8,128)}) %all-reduce.14.cloned.1.call-update) | async-done | bytes 262160 | tf_op jit(solution)/shard_map/psum | solution.py:47
  630.1 11.7 %cholesky.206 = f32[128,128]{1,0:T(8,128)S(1)} custom-call(f32[128,128]{1,0:T(8,128)S(1)} %cholesky.273), custom_call_target="Cholesky" | custom-call | tf_op jit(solution)/shard_map/jit(cholesky)/cholesky | solution.py:16
  652.2 11.7 %cholesky.223 = f32[128,128]{1,0:T(8,128)S(1)} custom-call(f32[128,128]{1,0:T(8,128)S(1)} %convolution_subtract_fusion.4), custom_call_target="Cholesky" | custom-call | tf_op jit(solution)/shard_map/jit(cholesky)/cholesky | solution.py:16
  670.3 19.7 %custom-call.15 = f32[2,128,128]{1,2,0:T(8,128)S(1)} custom-call(f32[2,128,128]{2,1,0:T(8,128)S(1)} %get-tuple-element.19), custom_call_target="InvertDiagBlocksLowerTriangular" | custom-call | tf_op jit(solution)/shard_map/jit(_solve_triangular)/triangular_solve | solution.py:20
  690.0 10.8 %fusion.3 = f32[128,16384]{1,0:T(8,128)S(1)} fusion(f32[256,16384]{0,1:T(8,128)} %bitcast.113, f32[2,128,128]{1,2,0:T(8,128)S(1)} %custom-call.15), kind=kOutput, calls=%fused_computation.12 | convolution fusion | flops 3221225472 | bytes 16842752 | tf_op jit(solution)/shard_map/jit(_solve_triangular)/triangular_solve | solution.py:20
  700.8 13.4 %convolution_subtract_fusion = f32[128,16384]{0,1:T(8,128)S(1)} fusion(f32[128,16384]{1,0:T(8,128)S(1)} %fusion.3, f32[256,16384]{0,1:T(8,128)S(1)} %bitcast.114, f32[256,256]{1,0:T(8,128)S(1)} %get-tuple-element.225), kind=kOutput, calls=%fused_computation.7 | convolution fusion | flops 3223322624 | bytes 25231360 | tf_op jit(solution)/shard_map/jit(_solve_triangular)/triangular_solve | solution.py:20
  724.0 13.7 %fusion.1 = f32[512,256]{1,0:T(8,128)} fusion(bf16[512,16384]{1,0:T(8,128)(2,1)} %copy-done.2, f32[128,16384]{1,0:T(8,128)} %fusion.19, f32[128,16384]{1,0:T(8,128)} %copy-done.1), kind=kOutput, calls=%fused_computation.11 | convolution fusion | flops 4311744512 | bytes 34078720 | tf_op jit(solution)/shard_map/dot_general | solution.py:35
  737.8 28.8 %all-reduce.16.cloned.1.call-done = f32[512,256]{1,0:T(8,128)} async-done(((f32[512,256]{1,0:T(8,128)}), f32[512,256]{1,0:T(8,128)}) %all-reduce.16.cloned.1.call-update) | async-done | bytes 524304 | tf_op jit(solution)/shard_map/psum | solution.py:35
  769.5 12.1 %multiply_bitcast_fusion = f32[16384,256]{0,1:T(8,128)} fusion(f32[128,16384]{1,0:T(8,128)} %fusion.19, f32[128,16384]{1,0:T(8,128)} %copy-done.1), kind=kLoop, calls=%fused_computation.9 | loop fusion | flops 8388608 | bytes 33554432 | tf_op jit(solution)/shard_map/mul | solution.py:54
  781.6 17.5 %copy.22 = f32[16384,256]{1,0:T(8,128)} copy(f32[16384,256]{0,1:T(8,128)} %multiply_bitcast_fusion) | data formatting | bytes 33554432
  799.2 61.0 %all-reduce.18.cloned.1.call-done = f32[256,256]{0,1:T(8,128)} async-done(((f32[256,256]{0,1:T(8,128)}), f32[256,256]{0,1:T(8,128)}) %all-reduce.18.cloned.1.call-update) | async-done | bytes 262160 | tf_op jit(solution)/shard_map/psum | solution.py:36
  862.2 11.7 %cholesky.240 = f32[128,128]{1,0:T(8,128)S(1)} custom-call(f32[128,128]{1,0:T(8,128)S(1)} %cholesky.276), custom_call_target="Cholesky" | custom-call | tf_op jit(solution)/shard_map/jit(cholesky)/cholesky | solution.py:16
  884.3 11.7 %cholesky.257 = f32[128,128]{1,0:T(8,128)S(1)} custom-call(f32[128,128]{1,0:T(8,128)S(1)} %convolution_subtract_fusion.3), custom_call_target="Cholesky" | custom-call | tf_op jit(solution)/shard_map/jit(cholesky)/cholesky | solution.py:16
  902.9 20.0 %custom-call.23 = f32[2,128,128]{1,2,0:T(8,128)S(1)} custom-call(f32[2,128,128]{2,1,0:T(8,128)S(1)} %get-tuple-element.27), custom_call_target="InvertDiagBlocksLowerTriangular" | custom-call | tf_op jit(solution)/shard_map/jit(_solve_triangular)/triangular_solve | solution.py:20
  (96 shorter events, 105.6 us)
Async XLA Ops:
  7.2 85.9 %all-reduce.8.cloned.1.call-start = ((), (), s32[]{:S(2)}) async-start(), calls=%async_computation | async-start | bytes 1048576 | tf_op jit(solution)/shard_map/psum | solution.py:35
  53.0 6.2 copy-start.2
  67.0 119.8 %all-reduce.10.cloned.1.call-start = ((), (), s32[]{:S(2)}) async-start(), calls=%async_computation.1 | async-start | bytes 524288 | tf_op jit(solution)/shard_map/psum | solution.py:36
  96.0 471.1 %all-reduce.12.cloned.1.call-start = ((), (), s32[]{:S(2)}) async-start(), calls=%async_computation.2 | async-start | bytes 33554432 | tf_op jit(solution)/shard_map/psum | solution.py:46
  268.5 359.5 %all-reduce.14.cloned.1.call-start = ((), (), s32[]{:S(2)}) async-start(), calls=%async_computation.3 | async-start | bytes 524288 | tf_op jit(solution)/shard_map/psum | solution.py:47
  605.0 161.6 %all-reduce.16.cloned.1.call-start = ((), (), s32[]{:S(2)}) async-start(), calls=%async_computation.4 | async-start | bytes 1048576 | tf_op jit(solution)/shard_map/psum | solution.py:35
  690.0 10.8 %copy-start = (f32[16384,256]{1,0:T(8,128)S(1)}, f32[16384,256]{1,0:T(8,128)}, u32[]{:S(2)}) copy-start(f32[16384,256]{1,0:T(8,128)} %all-reduce.12.cloned.1.call-done) | copy-start | bytes 50331652
  700.8 13.4 %copy-start.1 = (f32[128,16384]{1,0:T(8,128)}, f32[128,16384]{1,0:T(8,128)S(1)}, u32[]{:S(2)}) copy-start(f32[128,16384]{1,0:T(8,128)S(1)} %fusion.3) | copy-start | bytes 25165828
  737.7 122.4 %all-reduce.18.cloned.1.call-start = ((), (), s32[]{:S(2)}) async-start(), calls=%async_computation.5 | async-start | bytes 524288 | tf_op jit(solution)/shard_map/psum | solution.py:36
  781.6 141.2 %copy-start.3 = (f32[512,256]{1,0:T(8,128)S(1)}, f32[512,256]{1,0:T(8,128)}, u32[]{:S(2)}) copy-start(f32[512,256]{1,0:T(8,128)} %all-reduce.16.cloned.1.call-done) | copy-start | bytes 1572868
Sparse Core Ops, SparseCore 0:
  67.1 25.9 all-reduce.7
  97.0 89.7 all-reduce.9
  268.7 298.4 all-reduce.11
  605.1 22.9 all-reduce.13
  737.9 28.6 all-reduce.15
  770.4 89.6 all-reduce.17
where the time goes:
time: 938 us; the launch traced here: 933 us
  waiting for transfers between devices  528 us (56%)
  other arithmetic  195 us (21%)
  matrix products  121 us (13%)
  local copies, waits for them, and re-layouts  40 us (4%)
  blocking collectives  28 us (3%)
  between operations  19.6 us (2%)
    psum x1, waiting for transfers between devices, per_device(): whole = lax.psum(partial_value, 'row')  299 us
    psum x2, waiting for transfers between devices, left_orth(): gram = lax.psum(gram_of(whole), 'row')  151 us
    another operation x20, other arithmetic, factor_of(): return jnp.linalg.cholesky(gram)  103 us
    another operation x7, other arithmetic, solve_rows(): return jax.scipy.linalg.solve_triangular(lower, matrix.T, lower=True).T  59.4 us
    psum x2, waiting for transfers between devices, left_orth(): lax.psum(jnp.dot(table, rhs, preferred_element_type=jnp.float32), 'col')  54.8 us
    dot_general x3, matrix products, gram_of(): return jnp.dot(matrix.T, matrix, precision=lax.Precision.HIGHEST)  43.6 us
    another operation x9, matrix products, solve_rows(): return jax.scipy.linalg.solve_triangular(lower, matrix.T, lower=True).T  38.7 us
    unnamed x10, local copies, waits for them, and re-layouts  24.7 us
  transfers between devices with their start and end apart: 6, of which 6 were waited for; matrix products, arithmetic and copies ran while one was open for 3% of the time, Pallas kernels for 0%

commit v1 on v0

--- a/solution.py
+++ b/solution.py
@@ -2,6 +2,7 @@
 import jax.numpy as jnp
 from jax import lax
 from jax.sharding import PartitionSpec as P
+from jax.lax import axis_size, ppermute
 
 
 def lift(block, row_part, col_part, total):
@@ -43,7 +44,12 @@
     partial_value = lax.dot_general(
         table, q_first, (((0,), (0,)), ((), ())), preferred_element_type=jnp.float32
     )
-    whole = lax.psum(partial_value, "row")
+    workers = axis_size("row")
+    whole = partial_value
+    for it in [
+        [(to_i, to_i ^ idx) for to_i in range(workers)] for idx in (1, 2, 4, 8, 16) if idx < workers
+    ]:
+        whole = whole + ppermute(whole, axis_name="row", perm=it)
     gram = lax.psum(gram_of(whole), "col")
     q_second = solve_rows(factor_of(gram), whole)
     q_third = left_orth(q_second.astype(jnp.bfloat16), False)

time: 938 us -> 2150 us (2.29)
  waiting for transfers between devices: 528 us -> 1680 us
  other arithmetic: 195 us -> 248 us
    ppermute x0 -> x4, waiting for transfers between devices: none -> 1470 us  [per_device(): whole = whole + ppermute(whole, axis_name='row', perm=it)]
    psum x1 -> x0, waiting for transfers between devices: 299 us -> none  [per_device(): whole = lax.psum(partial_value, 'row')]
    add x0 -> x3, other arithmetic: none -> 34.9 us  [per_device(): whole = whole + ppermute(whole, axis_name='row', perm=it)]
  transfers between devices with their start and end apart: 6 -> 9, of which waited for: 6 -> 9; matrix products, arithmetic and copies ran while one was open for 3% -> 2% of each run, Pallas kernels for 0% -> 0%
where the time goes in v1:
time: 2150 us; the launch traced here: 2140 us
  waiting for transfers between devices  1680 us (78%)
  other arithmetic  248 us (12%)
  matrix products  118 us (5%)
  local copies, waits for them, and re-layouts  43.5 us (2%)
  blocking collectives  28 us (1%)
    ppermute x4, waiting for transfers between devices, per_device(): whole = whole + ppermute(whole, axis_name='row', perm=it)  1470 us
    psum x2, waiting for transfers between devices, left_orth(): gram = lax.psum(gram_of(whole), 'row')  152 us
    another operation x20, other arithmetic, factor_of(): return jnp.linalg.cholesky(gram)  103 us
    another operation x7, other arithmetic, solve_rows(): return jax.scipy.linalg.solve_triangular(lower, matrix.T, lower=True).T  59.8 us
    psum x2, waiting for transfers between devices, left_orth(): lax.psum(jnp.dot(table, rhs, preferred_element_type=jnp.float32), 'col')  54.8 us
    dot_general x3, matrix products, gram_of(): return jnp.dot(matrix.T, matrix, precision=lax.Precision.HIGHEST)  48.2 us
  transfers between devices with their start and end apart: 9, of which 9 were waited for; matrix products, arithmetic and copies ran while one was open for 2% of the time, Pallas kernels for 0%

profile of v1, /device:TPU:0, one launch (start us, length us, event | category | flops | bytes accessed | tf_op | source)
XLA Modules:
  0.0 2141.1 jit_solution(7547308335067274617)
XLA Ops:
  13.4 22.5 %all_gather.7 = s32[16384]{0:T(1024)S(1)} all-gather(s32[1024]{0:T(1024)} %param.10), channel_id=1, replica_groups=mesh['row'=16,'col'=2] {'row'}, dimensions={0}, use_global_device_ids=true | all-gather | bytes 69632 | tf_op jit(solution)/shard_map/all_gather | solution.py:30
  35.9 17.1 select_convert_fusion
  67.0 26.0 %all-reduce.7.cloned.1.call-done = f32[512,256]{1,0:T(8,128)} async-done(((f32[512,256]{1,0:T(8,128)}), f32[512,256]{1,0:T(8,128)}) %all-reduce.7.cloned.1.call-update) | async-done | bytes 524304 | tf_op jit(solution)/shard_map/psum | solution.py:36
  96.2 90.6 %all-reduce.9.cloned.1.call-done = f32[256,256]{0,1:T(8,128)} async-done(((f32[256,256]{0,1:T(8,128)}), f32[256,256]{0,1:T(8,128)}) %all-reduce.9.cloned.1.call-update) | async-done | bytes 262160 | tf_op jit(solution)/shard_map/psum | solution.py:37
  210.9 11.7 cholesky.189
  229.2 19.7 custom-call.20
  261.0 24.9 %collective-permute-done = f32[16384,256]{1,0:T(8,128)} collective-permute-done((f32[16384,256]{1,0:T(8,128)S(1)}, f32[16384,256]{1,0:T(8,128)}, u32[]{:S(2)}, u32[]{:S(2)}) %collective-permute-start) | collective-permute-done | bytes 16777248 | tf_op jit(solution)/shard_map/ppermute | solution.py:52
  285.9 11.7 add.51
  298.2 362.2 %collective-permute-done.1 = f32[16384,256]{1,0:T(8,128)} collective-permute-done((f32[16384,256]{1,0:T(8,128)}, f32[16384,256]{1,0:T(8,128)}, u32[]{:S(2)}, u32[]{:S(2)}) %collective-permute-start.1) | collective-permute-done | bytes 16777248 | tf_op jit(solution)/shard_map/ppermute | solution.py:52
  674.5 359.8 %collective-permute-done.2 = f32[16384,256]{1,0:T(8,128)} collective-permute-done((f32[16384,256]{1,0:T(8,128)S(1)}, f32[16384,256]{1,0:T(8,128)}, u32[]{:S(2)}, u32[]{:S(2)}) %collective-permute-start.2) | collective-permute-done | bytes 16777248 | tf_op jit(solution)/shard_map/ppermute | solution.py:52
  1034.3 11.7 add.53
  1047.8 719.8 %collective-permute-done.3 = f32[16384,256]{1,0:T(8,128)} collective-permute-done((f32[16384,256]{1,0:T(8,128)}, f32[16384,256]{1,0:T(8,128)}, u32[]{:S(2)}, u32[]{:S(2)}) %collective-permute-start.3) | collective-permute-done | bytes 16777248 | tf_op jit(solution)/shard_map/ppermute | solution.py:52
  1767.6 42.4 %fusion.6 = f32[256,256]{0,1:T(8,128)} fusion(f32[16384,256]{1,0:T(8,128)} %add.53, f32[16384,256]{1,0:T(8,128)} %collective-permute-done.3), kind=kOutput, calls=%fused_computation.16 | convolution fusion | flops 12889096192 | bytes 33816576 | tf_op jit(solution)/shard_map/dot_general | solution.py:25
  1810.1 18.1 add_bitcast_fusion
  1857.3 11.7 cholesky.223
  1875.3 20.1 custom-call.15
  1909.2 13.3 fusion.21
  1932.9 13.7 fusion.1
  1946.7 28.8 %all-reduce.13.cloned.1.call-done = f32[512,256]{1,0:T(8,128)} async-done(((f32[512,256]{1,0:T(8,128)}), f32[512,256]{1,0:T(8,128)}) %all-reduce.13.cloned.1.call-update) | async-done | bytes 524304 | tf_op jit(solution)/shard_map/psum | solution.py:36
  1978.4 12.1 multiply_bitcast_fusion
  1990.5 17.5 copy.22
  2008.0 61.0 %all-reduce.15.cloned.1.call-done = f32[256,256]{0,1:T(8,128)} async-done(((f32[256,256]{0,1:T(8,128)}), f32[256,256]{0,1:T(8,128)}) %all-reduce.15.cloned.1.call-update) | async-done | bytes 262160 | tf_op jit(solution)/shard_map/psum | solution.py:37
  2093.8 11.7 cholesky.257
  2111.8 19.9 custom-call.23
  (112 shorter events, 185.9 us)
Async XLA Ops:
  7.2 85.9 %all-reduce.7.cloned.1.call-start = ((), (), s32[]{:S(2)}) async-start(), calls=%async_computation | async-start | bytes 1048576 | tf_op jit(solution)/shard_map/psum | solution.py:36
  53.0 6.2 copy-start.1
  67.0 119.8 %all-reduce.9.cloned.1.call-start = ((), (), s32[]{:S(2)}) async-start(), calls=%async_computation.1 | async-start | bytes 524288 | tf_op jit(solution)/shard_map/psum | solution.py:37
  96.0 1736.5 %all-reduce.11.cloned.1.call-start = ((), (), s32[]{:S(2)}) async-start(), calls=%async_computation.2 | async-start | bytes 524288 | tf_op jit(solution)/shard_map/psum | solution.py:53
  260.5 25.4 %collective-permute-start = (f32[16384,256]{1,0:T(8,128)S(1)}, f32[16384,256]{1,0:T(8,128)}, u32[]{:S(2)}, u32[]{:S(2)}) collective-permute-start(f32[16384,256]{1,0:T(8,128)S(1)} %fusion.9), channel_id=1, source_target_pairs={{0,2},{2,0},{4,6},{6,4},{8,10},{10,8},{12,14},{14,12},{16,18},{18,... | collective-permute-start | bytes 50331656 | tf_op jit(solution)/shard_map/ppermute | solution.py:52
  297.6 362.8 %collective-permute-start.1 = (f32[16384,256]{1,0:T(8,128)}, f32[16384,256]{1,0:T(8,128)}, u32[]{:S(2)}, u32[]{:S(2)}) collective-permute-start(f32[16384,256]{1,0:T(8,128)} %add.51), channel_id=1, source_target_pairs={{0,4},{2,6},{4,0},{6,2},{8,12},{10,14},{12,8},{14,10},{16,20},{18,... | collective-permute-start | bytes 50331656 | tf_op jit(solution)/shard_map/ppermute | solution.py:52
  671.9 362.4 %collective-permute-start.2 = (f32[16384,256]{1,0:T(8,128)S(1)}, f32[16384,256]{1,0:T(8,128)}, u32[]{:S(2)}, u32[]{:S(2)}) collective-permute-start(f32[16384,256]{1,0:T(8,128)S(1)} %add.52), channel_id=1, source_target_pairs={{0,8},{2,10},{4,12},{6,14},{8,0},{10,2},{12,4},{14,6},{16,24},{18,... | collective-permute-start | bytes 50331656 | tf_op jit(solution)/shard_map/ppermute | solution.py:52
  1046.0 721.6 %collective-permute-start.3 = (f32[16384,256]{1,0:T(8,128)}, f32[16384,256]{1,0:T(8,128)}, u32[]{:S(2)}, u32[]{:S(2)}) collective-permute-start(f32[16384,256]{1,0:T(8,128)} %add.53), channel_id=1, source_target_pairs={{0,16},{2,18},{4,20},{6,22},{8,24},{10,26},{12,28},{14,30},{16,0},... | collective-permute-start | bytes 50331656 | tf_op jit(solution)/shard_map/ppermute | solution.py:52
  1810.0 165.5 %all-reduce.13.cloned.1.call-start = ((), (), s32[]{:S(2)}) async-start(), calls=%async_computation.3 | async-start | bytes 1048576 | tf_op jit(solution)/shard_map/psum | solution.py:36
  1895.4 27.2 %slice-start = ((s8[16777216]{0:T(1024)(128)(4,1)}), s8[4194304]{0:T(1024)(128)(4,1)S(1)}, s32[]{:S(2)}) async-start(s8[16777216]{0:T(1024)(128)(4,1)} %bitcast.111), calls=%async_computation.5 | async-start | bytes 8388608
  1895.4 27.2 %slice-start.1 = ((s8[16777216]{0:T(1024)(128)(4,1)}), s8[4194304]{0:T(1024)(128)(4,1)S(1)}, s32[]{:S(2)}) async-start(s8[16777216]{0:T(1024)(128)(4,1)} %bitcast.111), calls=%async_computation.6 | async-start | bytes 8388608
  1906.0 3.2 copy-start
  1909.2 13.4 slice-start.2
  1909.2 13.4 slice-start.3
  1946.7 122.4 %all-reduce.15.cloned.1.call-start = ((), (), s32[]{:S(2)}) async-start(), calls=%async_computation.4 | async-start | bytes 524288 | tf_op jit(solution)/shard_map/psum | solution.py:37
  1990.5 141.2 %copy-start.2 = (f32[512,256]{1,0:T(8,128)S(1)}, f32[512,256]{1,0:T(8,128)}, u32[]{:S(2)}) copy-start(f32[512,256]{1,0:T(8,128)} %all-reduce.13.cloned.1.call-done) | copy-start | bytes 1572868
Sparse Core Ops, SparseCore 0:
  67.1 25.9 all-reduce.6
  97.0 89.7 all-reduce.8
  1810.1 22.3 all-reduce.10
  1946.8 28.6 all-reduce.12
  1979.3 89.6 all-reduce.14
